TPU v7x, 32 devices: a whole 2x2x4 slice. The times are simulated.
32 devices in a mesh: groups: 2 (over x), wide: 16 (over z, y, core).
Axes of the slice: x: 2, y: 2, z: 4, core: 2. Of those that a mesh axis runs over, the one named last changes fastest.
Arguments:
- video: bfloat16 [64, 1024, 1152], P(('groups', 'wide')), parts along dimension 0, may hold values from -40 to 40
- modulation: float32 [12, 1152], P('groups'), parts along dimension 0, may hold values from -3 to 3
- spatial_input: bfloat16 [1152, 3456], replicated, may hold values from -1 to 1
- spatial_output: bfloat16 [1152, 1152], replicated, may hold values from -0.1875 to 0.1875
- temporal_input: bfloat16 [1152, 3456], replicated, may hold values from -1 to 1
- temporal_output: bfloat16 [1152, 1152], replicated, may hold values from -0.1875 to 0.1875
Outputs:
- refined: bfloat16 [64, 1024, 1152], P(('groups', 'wide')), parts along dimension 0
There are 2 independent parts, one for each index of `groups`. A program takes and returns all parts, laid end to end along the dimension named above; an argument that names none is the same for every part. Nothing has to cross between parts.
All inputs are finite; a program needn't handle non-finite values.
Results may differ from a plain program's by a relative error of at most 0.0052.
Values may be sent and summed in bfloat16 or wider, within the bound.
No kernel may reach another device: no remote copies, remote signals or barrier semaphores. Data moves between devices by JAX's collectives and lax.ppermute only.
A program may use at most 320 MiB of HBM per device.

v0:
```python
import math
import jax
import jax.numpy as jnp
from jax import lax
from jax.sharding import PartitionSpec as P

HEADS = 16
HEAD_DIM = 72
epsilon = 1e-06


def normalize(stream, offset_row, stretch):
    values = stream.astype(jnp.float32)
    average = jnp.mean(values, axis=-1, keepdims=True)
    centered = values - average
    spread = jnp.mean(centered * centered, axis=-1, keepdims=True)
    return (centered * lax.rsqrt(spread + epsilon) * (1.0 + stretch) + offset_row).astype(
        jnp.bfloat16
    )


def attend_space(video, modulation, spatial_input, spatial_output):
    count_local, length, features = video.shape
    score_scale = 1.0 / math.sqrt(HEAD_DIM)
    normed = normalize(video, modulation[0], modulation[1])
    triples = jnp.dot(
        normed.reshape(count_local * length, features),
        spatial_input,
        preferred_element_type=jnp.float32,
    )
    triples = triples.astype(jnp.bfloat16).reshape(count_local, length, 3, HEADS, HEAD_DIM)
    scores = (
        jnp.einsum(
            "fqhd,fkhd->fhqk",
            triples[:, :, 0],
            triples[:, :, 1],
            preferred_element_type=jnp.float32,
        )
        * score_scale
    )
    weights = jax.nn.softmax(scores, axis=-1).astype(jnp.bfloat16)
    attended = jnp.einsum(
        "fhqk,fkhd->fqhd", weights, triples[:, :, 2], preferred_element_type=jnp.float32
    ).astype(jnp.bfloat16)
    branch = jnp.dot(
        attended.reshape(count_local * length, features),
        spatial_output,
        preferred_element_type=jnp.float32,
    )
    return (
        video.astype(jnp.float32) + modulation[2] * branch.reshape(count_local, length, features)
    ).astype(jnp.bfloat16)


def attend_time(triples):
    frames, sites, triple_width = triples.shape
    score_scale = 1.0 / math.sqrt(HEAD_DIM)
    split_rows = triples.reshape(frames, sites, 3, HEADS, HEAD_DIM)
    scores = (
        jnp.einsum(
            "fshd,gshd->shfg",
            split_rows[:, :, 0],
            split_rows[:, :, 1],
            preferred_element_type=jnp.float32,
        )
        * score_scale
    )
    weights = jax.nn.softmax(scores, axis=-1).astype(jnp.bfloat16)
    attended = jnp.einsum(
        "shfg,gshd->fshd", weights, split_rows[:, :, 2], preferred_element_type=jnp.float32
    )
    return attended.astype(jnp.bfloat16).reshape(frames, sites, triple_width // 3)


def on_device(video, modulation, spatial_input, spatial_output, temporal_input, temporal_output):
    halfway = attend_space(video, modulation, spatial_input, spatial_output)
    count_local, length, features = halfway.shape
    devices = lax.axis_size("wide")
    per_device = length // devices
    normed = normalize(halfway, modulation[3], modulation[4])
    triples = jnp.dot(
        normed.reshape(count_local * length, features),
        temporal_input,
        preferred_element_type=jnp.float32,
    )
    triples = triples.astype(jnp.bfloat16).reshape(count_local, devices, per_device, 3 * features)
    attended = attend_time(
        lax.all_to_all(triples, "wide", split_axis=1, concat_axis=0, tiled=True)[:, 0]
    )[:, None]
    returned = lax.all_to_all(attended, "wide", split_axis=0, concat_axis=1, tiled=True)
    branch = jnp.dot(
        returned.reshape(count_local * length, features),
        temporal_output,
        preferred_element_type=jnp.float32,
    )
    result = halfway.astype(jnp.float32) + modulation[5] * branch.reshape(
        count_local, length, features
    )
    return result.astype(jnp.bfloat16)


def solution(mesh):
    placed = (P(("groups", "wide"), None, None), P("groups", None), P(), P(), P(), P())
    return jax.shard_map(
        on_device,
        mesh=mesh,
        in_specs=placed,
        out_specs=P(("groups", "wide"), None, None),
        check_vma=False,
    )
```

profile of v0, /device:TPU:1, one launch (start us, length us, event | category | flops | bytes accessed | tf_op | source)
XLA Modules:
  0.0 860.9 jit_solution(17176309826605197174)
XLA Ops:
  0.0 3.2 convert_reduce_fusion.1
  3.2 4.5 fusion.20
  7.7 0.7 slice_reduce_fusion.1
  8.4 0.0 copy-done.2
  8.4 1.9 fusion.23
  10.3 21.3 %convolution_convert_fusion.1 = bf16[2048,3456]{1,0:T(8,128)(2,1)} fusion(bf16[2048,1152]{1,0:T(8,128)(2,1)S(1)} %bitcast.82, bf16[1152,3456]{1,0:T(8,128)(2,1)S(1)} %copy-done.9), kind=kOutput, calls=%fused_computation.12 | convolution fusion | flops 16314531840 | bytes 26836992 | tf_op jit(solution)/shard_map/dot_general | solution.py:26
  31.6 49.4 %reshape.74 = bf16[2,1024,3,16,72]{4,3,2,1,0:T(8,128)(2,1)} reshape(bf16[2048,3456]{1,0:T(8,128)(2,1)} %convolution_convert_fusion.1) | data formatting | bytes 28311552 | tf_op jit(solution)/shard_map/reshape | solution.py:31
  81.0 17.1 %fusion.50 = (bf16[2,1024,1,16,72]{4,3,2,1,0:T(8,128)(2,1)}, bf16[2,1024,1,16,72]{4,3,2,1,0:T(8,128)(2,1)}, bf16[2,1024,1,16,72]{4,3,2,1,0:T(8,128)(2,1)}) fusion(bf16[2,1024,3,16,72]{4,3,2,1,0:T(8,128)(2,1)} %reshape.74), kind=kLoop, calls=%fused_computation.65 | loop fusion | bytes 28311552 | tf_op jit(solution)/shard_map/slice | solution.py:43
  98.1 11.5 %copy.45 = bf16[2,1024,1,16,72]{1,4,3,0,2:T(8,128)(2,1)} copy(bf16[2,1024,1,16,72]{4,3,2,1,0:T(8,128)(2,1)} %get-tuple-element.14) | data formatting | bytes 9437184
  109.6 11.5 %copy.46 = bf16[2,1024,1,16,72]{1,4,3,0,2:T(8,128)(2,1)} copy(bf16[2,1024,1,16,72]{4,3,2,1,0:T(8,128)(2,1)} %get-tuple-element.15) | data formatting | bytes 9437184
  121.1 11.5 %copy.47 = bf16[2,1024,1,16,72]{1,4,3,0,2:T(8,128)(2,1)} copy(bf16[2,1024,1,16,72]{4,3,2,1,0:T(8,128)(2,1)} %get-tuple-element.16) | data formatting | bytes 9437184
  132.6 52.3 %fusion.51 = (f32[2,16,1024]{2,1,0:T(8,128)S(1)}, f32[2,16,1024,1024]{2,3,1,0:T(8,128)}) fusion(bf16[2,1024,1,16,72]{1,4,3,0,2:T(8,128)(2,1)} %copy.47, bf16[2,1024,1,16,72]{1,4,3,0,2:T(8,128)(2,1)} %copy.46), kind=kOutput, calls=%fused_computation.66 | convolution fusion | flops 4932502528 | bytes 143785984 | tf_op jit(solution)/shard_map/sub | solution.py:41
  184.9 44.9 %fusion.42 = bf16[2,16,72,1024]{3,2,1,0:T(8,128)(2,1)} fusion(f32[2,16,1024,1024]{2,3,1,0:T(8,128)} %get-tuple-element.18, f32[2,16,1024]{2,1,0:T(8,128)S(1)} %get-tuple-element.17, bf16[2,1024,1,16,72]{1,4,3,0,2:T(8,128)(2,1)} %copy.45), kind=kOutput, calls=%fused_computation.49 | convolution fusion | flops 4901306368 | bytes 143785984 | tf_op jit(solution)/shard_map/fhqk,fkhd->fqhd/dot_general | solution.py:42
  229.8 22.1 %convert_reduce_fusion = (f32[2,1024]{1,0:T(2,128)S(1)}, bf16[2,1024,1152]{2,1,0:T(8,128)(2,1)S(1)}) fusion(bf16[2,1024,1152]{1,2,0:T(8,128)(2,1)} %bitcast.85, bf16[1152,1152]{1,0:T(8,128)(2,1)S(1)} %copy-done, f32[1152]{0:T(1024)S(1)} %copy-done.8, bf16[2,1024,1152]{2,1,0:T(8,128)(2,1)} %param.6), kind=kOutput, calls=%fused_computation.17 | convolution fusion | flops 5449971712 | bytes 16822784 | tf_op jit(solution)/shard_map/dot_general | solution.py:45
  251.9 0.0 copy-start.3
  251.9 1.4 fusion.16
  253.3 0.7 copy-done.3
  254.1 1.9 fusion.19
  256.0 22.0 %convolution_convert_fusion = bf16[2048,3456]{1,0:T(8,128)(2,1)S(1)} fusion(bf16[2048,1152]{1,0:T(8,128)(2,1)S(1)} %bitcast.83, bf16[1152,3456]{1,0:T(8,128)(2,1)} %param.10), kind=kOutput, calls=%fused_computation.11 | convolution fusion | flops 16314531840 | bytes 26836992 | tf_op jit(solution)/shard_map/dot_general | solution.py:81
  277.9 3.6 copy.32
  281.5 313.4 %all_to_all.30 = bf16[2,16,64,3456]{3,2,0,1:T(8,128)(2,1)} all-to-all(bf16[2,16,64,3456]{3,2,0,1:T(8,128)(2,1)S(1)} %copy.32), channel_id=1, replica_groups=mesh['groups'=2,'wide'=16] {'wide'}, dimensions={1} | all-to-all | bytes 28311552 | tf_op jit(solution)/shard_map/all_to_all | solution.py:88
  594.9 49.4 %reshape_squeeze.3 = bf16[32,64,3,16,72]{4,3,2,1,0:T(8,128)(2,1)} reshape(bf16[16,2,1,64,3456]{4,3,1,0,2:T(8,128)(2,1)} %bitcast.76) | data formatting | bytes 28311552 | tf_op jit(solution)/shard_map/reshape;squeeze | solution.py:58
  644.3 17.5 %fusion.49 = (bf16[32,64,1,16,72]{4,3,2,1,0:T(8,128)(2,1)}, bf16[32,64,1,16,72]{4,3,2,1,0:T(8,128)(2,1)}, bf16[32,64,1,16,72]{4,3,2,1,0:T(8,128)(2,1)}) fusion(bf16[32,64,3,16,72]{4,3,2,1,0:T(8,128)(2,1)} %reshape_squeeze.3), kind=kLoop, calls=%fused_computation.64 | loop fusion | bytes 28311552 | tf_op jit(solution)/shard_map/slice | solution.py:70
  661.8 22.1 %fusion.27 = f32[64,16,32,32]{2,3,1,0:T(8,128)} fusion(bf16[32,64,1,16,72]{4,3,2,1,0:T(8,128)(2,1)} %get-tuple-element.13, bf16[32,64,1,16,72]{4,3,2,1,0:T(8,128)(2,1)} %get-tuple-element.12), kind=kOutput, calls=%fused_computation.37 | convolution fusion | flops 150994944 | bytes 13631488 | tf_op jit(solution)/shard_map/fshd,gshd->shfg/dot_general | solution.py:60
  683.8 19.3 %fusion.60 = (f32[64,16,32]{2,1,0:T(8,128)S(1)}, f32[64,16,32,32]{2,3,1,0:T(8,128)}) fusion(f32[64,16,32,32]{2,3,1,0:T(8,128)} %fusion.27), kind=kOutput, calls=%fused_computation.67 | output fusion | flops 4194335 | bytes 8519680 | tf_op jit(solution)/shard_map/sub | solution.py:68
  703.1 14.1 %convert_bitcast_fusion = bf16[32,64,16,72]{3,0,2,1:T(8,128)(2,1)} fusion(f32[64,16,32,32]{2,3,1,0:T(8,128)} %get-tuple-element.22, f32[64,16,32]{2,1,0:T(8,128)S(1)} %get-tuple-element.21, bf16[32,64,1,16,72]{4,3,2,1,0:T(8,128)(2,1)} %get-tuple-element.11), kind=kOutput, calls=%fused_computation.40 | convolution fusion | flops 155451392 | bytes 13762560 | tf_op jit(solution)/shard_map/shfg,gshd->fshd/dot_general | solution.py:69
  717.2 9.8 %copy.37 = bf16[32,64,16,72]{3,2,1,0:T(8,128)(2,1)} copy(bf16[32,64,16,72]{3,0,2,1:T(8,128)(2,1)} %convert_bitcast_fusion) | data formatting | bytes 9437184 | tf_op jit(solution)/shard_map/convert_element_type | solution.py:72
  727.1 13.8 %broadcast_in_dim_reshape.3 = bf16[32,1,64,1152]{3,2,0,1:T(8,128)(2,1)} reshape(bf16[32,64,16,72]{3,2,1,0:T(8,128)(2,1)} %copy.37) | data formatting | bytes 9437184 | tf_op jit(solution)/shard_map/broadcast_in_dim;reshape | solution.py:87
  740.8 110.0 %all_to_all.31 = bf16[32,1,64,1152]{3,2,1,0:T(8,128)(2,1)S(1)} all-to-all(bf16[32,1,64,1152]{3,2,1,0:T(8,128)(2,1)} %bitcast.77), channel_id=1, replica_groups=mesh['groups'=2,'wide'=16] {'wide'}, dimensions={0} | all-to-all | bytes 9437184 | tf_op jit(solution)/shard_map/all_to_all | solution.py:90
  850.9 0.4 copy.39
  851.3 0.6 slice-done.1
  851.9 8.6 fusion.25
  (27 shorter events, 0.1 us)
Async XLA Ops:
  0.0 229.8 %copy-start = (bf16[1152,1152]{1,0:T(8,128)(2,1)S(1)}, bf16[1152,1152]{1,0:T(8,128)(2,1)}, u32[]{:S(2)}) copy-start(bf16[1152,1152]{1,0:T(8,128)(2,1)} %param.9) | copy-start | bytes 7962628
  0.0 8.4 copy-start.2
  0.0 7.7 copy-start.6
  0.0 10.3 %copy-start.9 = (bf16[1152,3456]{1,0:T(8,128)(2,1)S(1)}, bf16[1152,3456]{1,0:T(8,128)(2,1)}, u32[]{:S(2)}) copy-start(bf16[1152,3456]{1,0:T(8,128)(2,1)} %param.8) | copy-start | bytes 23887876
  184.9 44.9 %copy-start.8 = (f32[1152]{0:T(1024)S(1)}, f32[1152]{0:T(1024)}, u32[]{:S(2)}) copy-start(f32[1152]{0:T(1024)} %get-tuple-element.8) | copy-start | bytes 13828
  229.8 24.3 %copy-start.4 = (f32[1152]{0:T(1024)S(1)}, f32[1152]{0:T(1024)}, u32[]{:S(2)}) copy-start(f32[1152]{0:T(1024)} %get-tuple-element.9) | copy-start | bytes 13828
  229.8 24.3 %copy-start.5 = (f32[1152]{0:T(1024)S(1)}, f32[1152]{0:T(1024)}, u32[]{:S(2)}) copy-start(f32[1152]{0:T(1024)} %get-tuple-element.10) | copy-start | bytes 13828
  251.9 2.2 copy-start.3
  740.8 110.5 %slice-start = ((s8[4718592]{0:T(1024)(128)(4,1)}), s8[4194304]{0:T(1024)(128)(4,1)S(1)}, s32[]{:S(2)}) async-start(s8[4718592]{0:T(1024)(128)(4,1)} %bitcast.78), calls=%async_computation.2 | async-start | bytes 8388608
  740.8 110.5 %copy-start.7 = (f32[1152]{0:T(1024)S(1)}, f32[1152]{0:T(1024)}, u32[]{:S(2)}) copy-start(f32[1152]{0:T(1024)} %get-tuple-element.5) | copy-start | bytes 13828
  740.8 110.5 %copy-start.10 = (bf16[1152,1152]{1,0:T(8,128)(2,1)S(1)}, bf16[1152,1152]{1,0:T(8,128)(2,1)}, u32[]{:S(2)}) copy-start(bf16[1152,1152]{1,0:T(8,128)(2,1)} %param.11) | copy-start | bytes 7962628
  850.9 1.0 slice-start.1
  851.9 8.6 copy-start.1
where the time goes:
time: 871 us; the launch traced here: 861 us
  blocking collectives  423 us (49%)
  matrix products  207 us (24%)
  local copies, waits for them, and re-layouts  197 us (23%)
  other arithmetic  32.9 us (4%)
    all_to_all x1, blocking collectives, on_device(): lax.all_to_all(triples, 'wide', split_axis=1, concat_axis=0, tiled=True)  313 us
    all_to_all x1, blocking collectives, on_device(): lax.all_to_all(attended, 'wide', split_axis=0, concat_axis=1, tiled=True)  110 us
    sub x1, matrix products, attend_space(): weights = jax.nn.softmax(scores, axis=-1).astype(jnp.bfloat16)  52.3 us
    another operation x1, local copies, waits for them, and re-layouts, attend_time(): split_rows = triples.reshape(frames, sites, 3, HEADS, HEAD_DIM)  49.4 us
    reshape x1, local copies, waits for them, and re-layouts, attend_space(): triples.astype(jnp.bfloat16)  49.4 us
    dot_general x1, matrix products, attend_space(): jnp.einsum('fhqk,fkhd->fqhd', weights, triples[:, :, 2], preferred_elemen...  44.9 us
    unnamed x29, local copies, waits for them, and re-layouts  35.9 us
    dot_general x1, matrix products, attend_space(): jnp.dot(attended.reshape(count_local * length, features), spatial_output,...  22.1 us

commit v1 on v0

--- a/solution.py
+++ b/solution.py
@@ -87,7 +87,10 @@
     attended = attend_time(
         lax.all_to_all(triples, "wide", split_axis=1, concat_axis=0, tiled=True)[:, 0]
     )[:, None]
-    returned = lax.all_to_all(attended, "wide", split_axis=0, concat_axis=1, tiled=True)
+    returned = jnp.concatenate(
+        lax.all_to_all(jnp.stack(jnp.split(attended, lax.axis_size("wide"), axis=0)), "wide", 0, 0),
+        axis=1,
+    )
     branch = jnp.dot(
         returned.reshape(count_local * length, features),
         temporal_output,

time: 871 us -> 913 us (1.048)
  local copies, waits for them, and re-layouts: 197 us -> 250 us
  matrix products: 207 us -> 196 us
    split x0 -> x17, local copies, waits for them, and re-layouts: none -> 35.8 us  [on_device(): jnp.split(attended, lax.axis_size('wide'), axis=0)]
    another operation x1 -> x17, local copies, waits for them, and re-layouts: 13.8 us -> 29.6 us  [on_device(): jnp.stack(jnp.split(attended, lax.axis_size('wide'), axis=0))]
    dot_general x1, matrix products: 22.1 us -> 10.6 us  [attend_space(): jnp.dot(attended.reshape(count_local * length, features), spatial_output,...]
    unnamed x29 -> x50, local copies, waits for them, and re-layouts: 35.9 us -> 46.9 us
    convert_element_type x1 -> x0, local copies, waits for them, and re-layouts: 9.83 us -> none  [attend_time(): attended.astype(jnp.bfloat16).reshape(frames, sites, triple_width // 3)]
where the time goes in v1:
time: 913 us; the launch traced here: 902 us
  blocking collectives  423 us (46%)
  local copies, waits for them, and re-layouts  250 us (27%)
  matrix products  196 us (21%)
  other arithmetic  33 us (4%)
    all_to_all x1, blocking collectives, on_device(): lax.all_to_all(triples, 'wide', split_axis=1, concat_axis=0, tiled=True)  313 us
    all_to_all x1, blocking collectives, on_device(): lax.all_to_all(jnp.stack(jnp.split(attended, lax.axis_size('wide'), axis=...  110 us
    sub x1, matrix products, attend_space(): weights = jax.nn.softmax(scores, axis=-1).astype(jnp.bfloat16)  52.5 us
    another operation x1, local copies, waits for them, and re-layouts, attend_time(): split_rows = triples.reshape(frames, sites, 3, HEADS, HEAD_DIM)  49.4 us
    reshape x1, local copies, waits for them, and re-layouts, attend_space(): triples.astype(jnp.bfloat16)  49.4 us
    unnamed x50, local copies, waits for them, and re-layouts  46.9 us
    dot_general x1, matrix products, attend_space(): jnp.einsum('fhqk,fkhd->fqhd', weights, triples[:, :, 2], preferred_elemen...  44.9 us
    split x17, local copies, waits for them, and re-layouts, on_device(): jnp.split(attended, lax.axis_size('wide'), axis=0)  35.8 us

profile of v1, /device:TPU:1, one launch (start us, length us, event | category | flops | bytes accessed | tf_op | source)
XLA Modules:
  0.0 902.4 jit_solution(11895633505284858421)
XLA Ops:
  0.0 3.2 convert_reduce_fusion.1
  3.2 4.5 fusion.20
  10.3 21.3 %convolution_convert_fusion.1 = bf16[2048,3456]{1,0:T(8,128)(2,1)} fusion(bf16[2048,1152]{1,0:T(8,128)(2,1)S(1)} %bitcast.108, bf16[1152,3456]{1,0:T(8,128)(2,1)S(1)} %copy-done.12), kind=kOutput, calls=%fused_computation.12 | convolution fusion | flops 16314531840 | bytes 26836992 | tf_op jit(solution)/shard_map/dot_general | solution.py:26
  31.6 49.4 %reshape.108 = bf16[2,1024,3,16,72]{4,3,2,1,0:T(8,128)(2,1)} reshape(bf16[2048,3456]{1,0:T(8,128)(2,1)} %convolution_convert_fusion.1) | data formatting | bytes 28311552 | tf_op jit(solution)/shard_map/reshape | solution.py:31
  81.0 17.1 %fusion.50 = (bf16[2,1024,1,16,72]{4,3,2,1,0:T(8,128)(2,1)}, bf16[2,1024,1,16,72]{4,3,2,1,0:T(8,128)(2,1)}, bf16[2,1024,1,16,72]{4,3,2,1,0:T(8,128)(2,1)}) fusion(bf16[2,1024,3,16,72]{4,3,2,1,0:T(8,128)(2,1)} %reshape.108), kind=kLoop, calls=%fused_computation.81 | loop fusion | bytes 28311552 | tf_op jit(solution)/shard_map/slice | solution.py:43
  98.1 11.5 %copy.46 = bf16[2,1024,1,16,72]{1,4,3,0,2:T(8,128)(2,1)} copy(bf16[2,1024,1,16,72]{4,3,2,1,0:T(8,128)(2,1)} %get-tuple-element.14) | data formatting | bytes 9437184
  109.6 11.5 %copy.47 = bf16[2,1024,1,16,72]{1,4,3,0,2:T(8,128)(2,1)} copy(bf16[2,1024,1,16,72]{4,3,2,1,0:T(8,128)(2,1)} %get-tuple-element.15) | data formatting | bytes 9437184
  121.1 11.5 %copy.48 = bf16[2,1024,1,16,72]{1,4,3,0,2:T(8,128)(2,1)} copy(bf16[2,1024,1,16,72]{4,3,2,1,0:T(8,128)(2,1)} %get-tuple-element.16) | data formatting | bytes 9437184
  132.6 52.5 %fusion.52 = (f32[2,16,1024]{2,1,0:T(8,128)S(1)}, f32[2,16,1024,1024]{2,3,1,0:T(8,128)}) fusion(bf16[2,1024,1,16,72]{1,4,3,0,2:T(8,128)(2,1)} %copy.48, bf16[2,1024,1,16,72]{1,4,3,0,2:T(8,128)(2,1)} %copy.47), kind=kOutput, calls=%fused_computation.83 | convolution fusion | flops 4932502528 | bytes 143785984 | tf_op jit(solution)/shard_map/sub | solution.py:41
  185.1 44.9 %fusion.42 = bf16[2,16,72,1024]{3,2,1,0:T(8,128)(2,1)} fusion(f32[2,16,1024,1024]{2,3,1,0:T(8,128)} %get-tuple-element.34, f32[2,16,1024]{2,1,0:T(8,128)S(1)} %get-tuple-element.33, bf16[2,1024,1,16,72]{1,4,3,0,2:T(8,128)(2,1)} %copy.46), kind=kOutput, calls=%fused_computation.49 | convolution fusion | flops 4901306368 | bytes 143785984 | tf_op jit(solution)/shard_map/fhqk,fkhd->fqhd/dot_general | solution.py:42
  230.0 10.6 %convert_reduce_fusion = (f32[2,1024]{1,0:T(2,128)S(1)}, bf16[2,1024,1152]{2,1,0:T(8,128)(2,1)S(1)}) fusion(bf16[2,1024,1152]{1,2,0:T(8,128)(2,1)} %bitcast.111, bf16[1152,1152]{1,0:T(8,128)(2,1)S(1)} %copy-done, f32[1152]{0:T(1024)S(1)} %copy-done.11, bf16[2,1024,1152]{2,1,0:T(8,128)(2,1)} %param.6), kind=kOutput, calls=%fused_computation.17 | convolution fusion | flops 5449971712 | bytes 16822784 | tf_op jit(solution)/shard_map/dot_general | solution.py:45
  244.7 22.0 %convolution_convert_fusion = bf16[2048,3456]{1,0:T(8,128)(2,1)S(1)} fusion(bf16[2048,1152]{1,0:T(8,128)(2,1)S(1)} %bitcast.109, bf16[1152,3456]{1,0:T(8,128)(2,1)} %param.10), kind=kOutput, calls=%fused_computation.11 | convolution fusion | flops 16314531840 | bytes 26836992 | tf_op jit(solution)/shard_map/dot_general | solution.py:81
  266.7 3.6 copy.19
  270.3 313.4 %all_to_all.20 = bf16[2,16,64,3456]{3,2,0,1:T(8,128)(2,1)} all-to-all(bf16[2,16,64,3456]{3,2,0,1:T(8,128)(2,1)S(1)} %copy.19), channel_id=1, replica_groups=mesh['groups'=2,'wide'=16] {'wide'}, dimensions={1} | all-to-all | bytes 28311552 | tf_op jit(solution)/shard_map/all_to_all | solution.py:88
  583.6 49.4 %reshape_squeeze.3 = bf16[32,64,3,16,72]{4,3,2,1,0:T(8,128)(2,1)} reshape(bf16[16,2,1,64,3456]{4,3,1,0,2:T(8,128)(2,1)} %bitcast.103) | data formatting | bytes 28311552 | tf_op jit(solution)/shard_map/reshape;squeeze | solution.py:58
  633.0 17.5 %fusion.49 = (bf16[32,64,1,16,72]{4,3,2,1,0:T(8,128)(2,1)}, bf16[32,64,1,16,72]{4,3,2,1,0:T(8,128)(2,1)}, bf16[32,64,1,16,72]{4,3,2,1,0:T(8,128)(2,1)}) fusion(bf16[32,64,3,16,72]{4,3,2,1,0:T(8,128)(2,1)} %reshape_squeeze.3), kind=kLoop, calls=%fused_computation.80 | loop fusion | bytes 28311552 | tf_op jit(solution)/shard_map/slice | solution.py:70
  650.5 22.1 %fusion.27 = f32[64,16,32,32]{2,3,1,0:T(8,128)} fusion(bf16[32,64,1,16,72]{4,3,2,1,0:T(8,128)(2,1)} %get-tuple-element.13, bf16[32,64,1,16,72]{4,3,2,1,0:T(8,128)(2,1)} %get-tuple-element.12), kind=kOutput, calls=%fused_computation.37 | convolution fusion | flops 150994944 | bytes 13631488 | tf_op jit(solution)/shard_map/fshd,gshd->shfg/dot_general | solution.py:60
  672.6 19.5 %fusion.61 = (f32[64,16,32]{2,1,0:T(8,128)S(1)}, f32[64,16,32,32]{2,3,1,0:T(8,128)}) fusion(f32[64,16,32,32]{2,3,1,0:T(8,128)} %fusion.27), kind=kOutput, calls=%fused_computation.84 | output fusion | flops 4194335 | bytes 8519680 | tf_op jit(solution)/shard_map/sub | solution.py:68
  692.1 14.1 %convert_bitcast_fusion = bf16[32,64,16,72]{3,0,2,1:T(8,128)(2,1)} fusion(f32[64,16,32,32]{2,3,1,0:T(8,128)} %get-tuple-element.38, f32[64,16,32]{2,1,0:T(8,128)S(1)} %get-tuple-element.37, bf16[32,64,1,16,72]{4,3,2,1,0:T(8,128)(2,1)} %get-tuple-element.11), kind=kOutput, calls=%fused_computation.40 | convolution fusion | flops 155451392 | bytes 13762560 | tf_op jit(solution)/shard_map/shfg,gshd->fshd/dot_general | solution.py:69
  706.2 16.7 %fusion.51 = (bf16[2,64,16,72]{3,0,2,1:T(2,128)(2,1)S(1)}, bf16[2,64,16,72]{3,0,2,1:T(2,128)(2,1)}, bf16[2,64,16,72]{3,0,2,1:T(2,128)(2,1)}, bf16[2,64,16,72]{3,...) fusion(bf16[32,64,16,72]{3,0,2,1:T(8,128)(2,1)} %convert_bitcas, ...), kind=kLoop, calls=%fused_computation.82 | loop fusion | bytes 9437184 | tf_op jit(solution)/shard_map/split | solution.py:91
  727.2 2.3 stack.65
  731.3 2.3 stack.64
  735.5 2.2 stack.63
  739.6 2.3 stack.62
  743.8 2.3 stack.61
  747.9 2.3 stack.60
  752.1 2.2 stack.59
  756.2 2.3 stack.58
  760.4 2.3 stack.57
  763.5 2.3 stack.56
  782.8 109.8 %all_to_all.21 = bf16[16,2,1,64,1152]{4,3,1,2,0:T(8,128)(2,1)S(1)} all-to-all(bf16[16,2,1,64,1152]{4,3,1,2,0:T(8,128)(2,1)S(1)} %constant_dynamic-update-slice_fusion), channel_id=1, replica_groups=mesh['groups'=2,'wide'=16] {'wide'}, dimensions={0} | all-to-all | bytes 9437184 | tf_op jit(solution)/shard_map/all_to_all | solution.py:91
  893.6 8.6 fusion.25
  (80 shorter events, 44.9 us)
Async XLA Ops:
  0.0 230.0 %copy-start = (bf16[1152,1152]{1,0:T(8,128)(2,1)S(1)}, bf16[1152,1152]{1,0:T(8,128)(2,1)}, u32[]{:S(2)}) copy-start(bf16[1152,1152]{1,0:T(8,128)(2,1)} %param.9) | copy-start | bytes 7962628
  0.0 8.4 copy-start.2
  0.0 7.7 copy-start.9
  0.0 10.3 %copy-start.12 = (bf16[1152,3456]{1,0:T(8,128)(2,1)S(1)}, bf16[1152,3456]{1,0:T(8,128)(2,1)}, u32[]{:S(2)}) copy-start(bf16[1152,3456]{1,0:T(8,128)(2,1)} %param.8) | copy-start | bytes 23887876
  185.1 44.9 %copy-start.11 = (f32[1152]{0:T(1024)S(1)}, f32[1152]{0:T(1024)}, u32[]{:S(2)}) copy-start(f32[1152]{0:T(1024)} %get-tuple-element.8) | copy-start | bytes 13828
  230.0 12.8 %copy-start.7 = (f32[1152]{0:T(1024)S(1)}, f32[1152]{0:T(1024)}, u32[]{:S(2)}) copy-start(f32[1152]{0:T(1024)} %get-tuple-element.9) | copy-start | bytes 13828
  230.0 12.8 %copy-start.8 = (f32[1152]{0:T(1024)S(1)}, f32[1152]{0:T(1024)}, u32[]{:S(2)}) copy-start(f32[1152]{0:T(1024)} %get-tuple-element.10) | copy-start | bytes 13828
  240.6 2.2 copy-start.3
  767.1 15.6 %copy-start.4 = (bf16[1,2,1,64,1152]{4,3,1,2,0:T(8,128)(2,1)S(1)}, bf16[1,2,1,64,1152]{4,3,1,2,0:T(8,128)(2,1)}, u32[]{:S(2)}) copy-start(bf16[1,2,1,64,1152]{4,3,1,2,0:T(8,128)(2,1)} %stack.65) | copy-start | bytes 884740
  768.4 10.2 %copy-start.5 = (bf16[1,2,1,64,1152]{4,3,1,2,0:T(8,128)(2,1)S(1)}, bf16[1,2,1,64,1152]{4,3,1,2,0:T(8,128)(2,1)}, u32[]{:S(2)}) copy-start(bf16[1,2,1,64,1152]{4,3,1,2,0:T(8,128)(2,1)} %stack.60) | copy-start | bytes 884740
  769.7 8.9 copy-start.6
  782.7 110.3 %slice-start = ((s8[4718592]{0:T(1024)(128)(4,1)}), s8[4194304]{0:T(1024)(128)(4,1)S(1)}, s32[]{:S(2)}) async-start(s8[4718592]{0:T(1024)(128)(4,1)} %bitcast.104), calls=%async_computation.2 | async-start | bytes 8388608
  782.8 110.3 %copy-start.10 = (f32[1152]{0:T(1024)S(1)}, f32[1152]{0:T(1024)}, u32[]{:S(2)}) copy-start(f32[1152]{0:T(1024)} %get-tuple-element.5) | copy-start | bytes 13828
  782.8 110.3 %copy-start.13 = (bf16[1152,1152]{1,0:T(8,128)(2,1)S(1)}, bf16[1152,1152]{1,0:T(8,128)(2,1)}, u32[]{:S(2)}) copy-start(bf16[1152,1152]{1,0:T(8,128)(2,1)} %param.11) | copy-start | bytes 7962628
  892.6 1.0 slice-start.1
  893.6 8.6 copy-start.1
